TPU v7x, 32 devices: a whole 2x2x4 slice. The times are simulated.
32 devices in a mesh: sx: 4 (over y, x), sy: 8 (over z, core).
Axes of the slice: x: 2, y: 2, z: 4, core: 2. Of those that a mesh axis runs over, the one named last changes fastest.
Arguments:
- forward_weights: float32 [4096, 8, 432], P(('sy', 'sx')), may hold values from -6 to 6
- adjoint_weights: float32 [32768, 432], P(('sx', 'sy')), may hold values from -6 to 6
- medium: float32 [4], replicated, may hold values from 0.2 to 0.6
Outputs:
- forward_out: float32 [32768, 432], P(('sx', 'sy'))
- adjoint_out: float32 [8, 4096, 432], P(None, ('sy', 'sx'))
All inputs are finite; a program needn't handle non-finite values.
Results may differ from a plain program's by a relative error of at most 0.0003.
Values sent between devices are 32-bit elements; how exact they have to be, the bound alone decides.
A program may use at most 128 MiB of HBM per device.

v0:
```python
import math

import jax
import jax.numpy as jnp
import numpy as np
from jax import lax
from jax.sharding import PartitionSpec as P

ORDER = 6
LEVELS = 4
Q = 216


two_pi = 2.0 * math.pi
shrink = 1.0 / math.sqrt(8.0)
band = 8.0


def cheb_points(order_count):
    return np.array(
        [
            (1.0 - math.cos((2 * node_index + 1) * math.pi / (2 * order_count))) / 2.0
            for node_index in range(order_count)
        ]
    )


def child_table(order_count):
    nodes_here = cheb_points(order_count)
    halves = []
    for offset_bit in range(2):
        matrix = np.zeros((order_count, order_count))
        for row_index in range(order_count):
            where_at = (nodes_here[row_index] + offset_bit) / 2.0
            for col_index in range(order_count):
                value_now = 1.0
                for other_index in range(order_count):
                    if other_index != col_index:
                        value_now *= (where_at - nodes_here[other_index]) / (
                            nodes_here[col_index] - nodes_here[other_index]
                        )
                matrix[row_index, col_index] = value_now
        halves.append(matrix)
    blocks_out = []
    for child_index in range(8):
        along_x = halves[child_index // 4]
        along_y = halves[child_index // 2 % 2]
        along_z = halves[child_index % 2]
        blocks_out.append(np.kron(np.kron(along_x, along_y), along_z))
    return jnp.asarray(np.stack(blocks_out), dtype=jnp.float32)


def box_digits(box_index, groups):
    coord_x = jnp.zeros_like(box_index)
    coord_y = jnp.zeros_like(box_index)
    coord_z = jnp.zeros_like(box_index)
    for group_now in range(groups):
        digit_now = box_index // 8 ** (groups - 1 - group_now) % 8
        coord_x = coord_x * 2 + digit_now // 4
        coord_y = coord_y * 2 + digit_now // 2 % 2
        coord_z = coord_z * 2 + digit_now % 2
    return jnp.stack([coord_x, coord_y, coord_z], axis=-1).astype(jnp.float32)


def box_centres(box_index, groups):
    return (box_digits(box_index, groups) + 0.5) / float(2**groups)


def box_points(box_index, groups):
    box_side = band / float(2**groups)
    nodes_here = jnp.asarray(cheb_points(ORDER), dtype=jnp.float32)
    grid_x = jnp.repeat(nodes_here, ORDER * ORDER)
    grid_y = jnp.tile(jnp.repeat(nodes_here, ORDER), ORDER)
    grid_z = jnp.tile(nodes_here, ORDER * ORDER)
    offsets = jnp.stack([grid_x, grid_y, grid_z], axis=-1)
    corner = box_digits(box_index, groups)
    return box_side * (corner[..., None, :] + offsets)


def phase_angle(centres, points, medium):
    along = jnp.sum(centres * points, axis=-1)
    radius = jnp.sqrt(jnp.sum(points * points, axis=-1))
    travel = medium[0] + jnp.sum(medium[1:] * centres, axis=-1)
    return two_pi * (along + travel * radius)


def complex_turn(real_part, imag_part, angle_now, sign_now):
    cosine = jnp.cos(angle_now)
    sine_part = sign_now * jnp.sin(angle_now)
    return (real_part * cosine - imag_part * sine_part, real_part * sine_part + imag_part * cosine)


def forward_level(weights, src_off, tgt_off, level_now, medium, interp):
    src_count, tgt_count = (weights.shape[0], weights.shape[1])
    shot_count, point_count = (weights.shape[3], weights.shape[4])
    parent_count = src_count // 8
    new_targets = tgt_off * 8 + jnp.arange(tgt_count * 8, dtype=jnp.int32)
    centres = box_centres(new_targets, level_now + 2).reshape(tgt_count, 8, 3)
    children = src_off + jnp.arange(src_count, dtype=jnp.int32)
    child_points = box_points(children, LEVELS - level_now).reshape(parent_count, 8, point_count, 3)
    parents = src_off // 8 + jnp.arange(parent_count, dtype=jnp.int32)
    parent_points = box_points(parents, LEVELS - level_now - 1)
    theta_in = phase_angle(
        centres[None, None, :, :, None, :], child_points[:, :, None, None, :, :], medium
    )
    theta_out = phase_angle(
        centres[None, :, :, None, :], parent_points[:, None, None, :, :], medium
    )
    shaped = weights.reshape(parent_count, 8, tgt_count, 1, 2, shot_count, point_count)
    turned = complex_turn(
        shaped[:, :, :, :, 0], shaped[:, :, :, :, 1], theta_in[:, :, :, :, None, :], 1.0
    )
    stacked = jnp.stack(turned, axis=4)
    mixed = jnp.einsum("pctkxhq,cqs->ptkxhs", stacked, interp, precision=lax.Precision.HIGHEST)
    result_re, result_im = complex_turn(
        mixed[:, :, :, 0], mixed[:, :, :, 1], theta_out[:, :, :, None, :], -1.0
    )
    output = shrink * jnp.stack([result_re, result_im], axis=3)
    return output.reshape(parent_count, tgt_count * 8, 2, shot_count, point_count)


def adjoint_level(values, tgt_off, src_off, level_now, medium, interp):
    tgt_count, src_count = (values.shape[0], values.shape[1])
    shot_count, point_count = (values.shape[3], values.shape[4])
    parent_count = tgt_count // 8
    targets = tgt_off + jnp.arange(tgt_count, dtype=jnp.int32)
    centres = box_centres(targets, level_now + 2).reshape(parent_count, 8, 3)
    sources = src_off + jnp.arange(src_count, dtype=jnp.int32)
    source_points = box_points(sources, LEVELS - level_now - 1)
    children = src_off * 8 + jnp.arange(src_count * 8, dtype=jnp.int32)
    child_points = box_points(children, LEVELS - level_now).reshape(src_count, 8, point_count, 3)
    theta_out = phase_angle(
        centres[:, :, None, None, :], source_points[None, None, :, :, :], medium
    )
    theta_in = phase_angle(
        centres[:, :, None, None, None, :], child_points[None, None, :, :, :, :], medium
    )
    shaped = values.reshape(parent_count, 8, src_count, 2, shot_count, point_count)
    turned = complex_turn(shaped[:, :, :, 0], shaped[:, :, :, 1], theta_out[:, :, :, None, :], 1.0)
    stacked = jnp.stack(turned, axis=3)
    spread = jnp.einsum("pkbxhs,cqs->pkbcxhq", stacked, interp, precision=lax.Precision.HIGHEST)
    back_re, back_im = complex_turn(
        spread[:, :, :, :, 0], spread[:, :, :, :, 1], theta_in[:, :, :, :, None, :], -1.0
    )
    output = shrink * jnp.stack([jnp.sum(back_re, axis=1), jnp.sum(back_im, axis=1)], axis=3)
    return output.reshape(parent_count, src_count * 8, 2, shot_count, point_count)


def flatten_pairs(array_now):
    return array_now.reshape(array_now.shape[0], array_now.shape[1], -1)


def unfold_pairs(array_now):
    return array_now.reshape(array_now.shape[0], array_now.shape[1], 2, -1, Q)


def forward_moved(state_in, moved_array, axis_index):
    array_now, src_off, tgt_off, level_now = state_in
    return (
        moved_array,
        src_off - axis_index * array_now.shape[0],
        tgt_off + axis_index * moved_array.shape[1],
        level_now,
    )


def adjoint_moved(state_in, moved_array, axis_index):
    array_now, tgt_off, src_off, level_now = state_in
    return (
        moved_array,
        tgt_off - axis_index * array_now.shape[0],
        src_off + axis_index * moved_array.shape[1],
        level_now,
    )


def forward_steps(state_in, operations, medium, interp, index_x):
    for operation in operations:
        array_now, src_off, tgt_off, level_now = state_in
        if operation == "level":
            state_in = (
                forward_level(array_now, src_off, tgt_off, level_now, medium, interp),
                src_off // 8,
                tgt_off * 8,
                level_now + 1,
            )
        else:
            moved_array = unfold_pairs(
                lax.all_to_all(
                    flatten_pairs(array_now), "sx", split_axis=1, concat_axis=0, tiled=True
                )
            )
            state_in = forward_moved(state_in, moved_array, index_x)
    return state_in


def adjoint_steps(state_in, operations, medium, interp, index_x):
    for operation in operations:
        array_now, tgt_off, src_off, level_now = state_in
        if operation == "level":
            state_in = (
                adjoint_level(array_now, tgt_off, src_off, level_now - 1, medium, interp),
                tgt_off // 8,
                src_off * 8,
                level_now - 1,
            )
        else:
            moved_array = unfold_pairs(
                lax.all_to_all(
                    flatten_pairs(array_now), "sx", split_axis=1, concat_axis=0, tiled=True
                )
            )
            state_in = adjoint_moved(state_in, moved_array, index_x)
    return state_in


def shards(forward_weights, adjoint_weights, medium):
    interp = child_table(ORDER)
    size_x = lax.axis_size("sx")
    size_y = lax.axis_size("sy")
    index_x = lax.axis_index("sx")
    index_y = lax.axis_index("sy")
    local_sources = forward_weights.shape[0]
    plan_ops = []
    remaining = [("sx", size_x), ("sy", size_y)]
    local_width = local_sources
    for level_now in range(LEVELS):
        while local_width < 8:
            axis_name, axis_size = remaining.pop(0)
            plan_ops.append(axis_name)
            local_width = local_width * axis_size
        plan_ops.append("level")
        local_width = local_width // 8
    cut_at = plan_ops.index("sy")
    early_ops = plan_ops[:cut_at]
    late_ops = plan_ops[cut_at + 1 :]
    forward_state = (
        unfold_pairs(forward_weights),
        (index_y * size_x + index_x) * local_sources,
        jnp.int32(0),
        0,
    )
    back_state = (
        unfold_pairs(adjoint_weights[:, None]),
        (index_x * size_y + index_y) * adjoint_weights.shape[0],
        jnp.int32(0),
        LEVELS,
    )
    forward_state = forward_steps(forward_state, early_ops, medium, interp, index_x)
    moved_forward = lax.all_to_all(
        flatten_pairs(forward_state[0]), "sy", split_axis=1, concat_axis=0, tiled=True
    )
    forward_state = forward_moved(forward_state, unfold_pairs(moved_forward), index_y)
    forward_state = forward_steps(forward_state, late_ops, medium, interp, index_x)
    back_state = adjoint_steps(back_state, list(reversed(late_ops)), medium, interp, index_x)
    moved_back = lax.all_to_all(
        flatten_pairs(back_state[0]), "sy", split_axis=1, concat_axis=0, tiled=True
    )
    back_state = adjoint_moved(back_state, unfold_pairs(moved_back), index_y)
    back_state = adjoint_steps(back_state, list(reversed(early_ops)), medium, interp, index_x)
    forward_out = forward_state[0].reshape(forward_state[0].shape[1], -1)
    return (forward_out, flatten_pairs(back_state[0]))


def solution(mesh):
    in_specs = (P(("sy", "sx"), None, None), P(("sx", "sy"), None), P())
    out_specs = (P(("sx", "sy"), None), P(None, ("sy", "sx"), None))
    return jax.shard_map(shards, mesh=mesh, in_specs=in_specs, out_specs=out_specs, check_vma=False)
```

profile of v0, /device:TPU:1, one launch (start us, length us, event | category | flops | bytes accessed | tf_op | source)
XLA Modules:
  0.0 692.4 jit_solution(13334778669593530293)
XLA Ops:
  33.0 7.2 %multiply_reduce_fusion.3 = f32[16,8,8,8,216]{4,3,2,1,0:T(8,128)S(1)} fusion(f32[16,8,216,3]{2,3,1,0:T(4,128)} %copy.383, f32[8,8,3]{1,2,0:T(4,128)} %copy.381), kind=kLoop, calls=%fused_computation.3 | loop fusion | flops 8847360 | bytes 7410432 | tf_op jit(solution)/shard_map/reduce_sum | solution.py:81
  45.4 32.7 %multiply_subtract_fusion.1 = (f32[16,8,8,8,1,1,216]{6,3,1,4,2,0,5:T(8,128)S(1)}, f32[16,8,8,8,1,1,216]{6,3,1,4,2,0,5:T(8,128)S(1)}) fusion(f32[16,8,8,8,216]{4,3,2,1,0:T(8,128)S(1)} %multiply_reduce_fusion.3, f32[16,8,8,216]{3,1,2,0:T(8,128)S(1)} %get-tuple-element.124, f32[16,8,216]{2,1,0:T(8,128)} %sqrt.128, f32[8,8]{1,0:T(8,128)S(1)} %broadcast_add_fusion.19, ...), kind=kLoop, calls=%fused_computation.48 | loop fusion | flops 15925248 | bytes 23113984 | tf_op jit(solution)/shard_map/sub | solution.py:90
  78.2 21.0 %fusion.40 = f32[16,8,8,2,1,216]{5,2,3,1,0,4:T(8,128)S(1)} fusion(f32[8,216,216,1,1,1]{2,1,0,5,4,3:T(8,128)S(1)} %copy-done.120, f32[16,8,8,8,1,1,216]{6,3,1,4,2,0,5:T(8,128)S(1)} %get-tuple-element.27, f32[16,8,8,8,1,1,216]{6,3,1,4,2,0,5:T(8,128)S(1)} %get-tuple-element.26), kind=kOutput, calls=%fused_computation.112 | convolution fusion | flops 9176481792 | bytes 17418240 | tf_op jit(solution)/shard_map/pctkxhq,cqs->ptkxhs/dot_general | solution.py:114
  108.5 7.8 %multiply_reduce_fusion.2 = f32[2,8,64,8,216]{4,3,2,1,0:T(8,128)} fusion(f32[2,8,216,3]{2,3,1,0:T(4,128)S(1)} %copy.392, f32[64,8,3]{1,2,0:T(4,128)S(1)} %copy.390), kind=kLoop, calls=%fused_computation.2 | loop fusion | flops 8847360 | bytes 7125504 | tf_op jit(solution)/shard_map/reduce_sum | solution.py:81
  120.3 33.2 %multiply_subtract_fusion = (f32[2,8,64,8,1,1,216]{6,3,1,4,2,0,5:T(8,128)S(1)}, f32[2,8,64,8,1,1,216]{6,3,1,4,2,0,5:T(8,128)S(1)}) fusion(f32[2,8,64,8,216]{4,3,2,1,0:T(8,128)} %multiply_reduce_fusion.2, f32[2,8,64,216]{3,1,2,0:T(8,128)S(1)} %copy.396, f32[2,8,216]{2,1,0:T(8,128)} %sqrt.130, f32[64,8]{1,0:T(8,128)} %copy.394, f32[2,8,64,216]{3,1,2,0:T(8,128)S(1)} %copy.389), kind=kLoop, calls=%fused_computation.46 | loop fusion | flops 15925248 | bytes 23019008 | tf_op jit(solution)/shard_map/sub | solution.py:90
  153.6 21.4 %fusion.39 = f32[2,64,8,2,1,216]{5,2,3,1,0,4:T(8,128)S(1)} fusion(f32[8,216,216,1,1,1]{2,1,0,5,4,3:T(8,128)S(1)} %copy-done.121, f32[2,8,64,8,1,1,216]{6,3,1,4,2,0,5:T(8,128)S(1)} %get-tuple-element.29, f32[2,8,64,8,1,1,216]{6,3,1,4,2,0,5:T(8,128)S(1)} %get-tuple-element.28), kind=kOutput, calls=%fused_computation.111 | convolution fusion | flops 9176481792 | bytes 17418240 | tf_op jit(solution)/shard_map/pctkxhq,cqs->ptkxhs/dot_general | solution.py:114
  230.2 5.3 fusion.660
  257.7 11.3 %convolution_bitcast_fusion.2 = f32[128,8,1,8,2,1,216]{0,6,4,1,3,5,2:T(8,128)S(1)} fusion(f32[8,216,216,1,1]{2,1,4,3,0:T(8,128)S(1)} %copy-done.11, f32[128,8,1,1,1,216]{0,5,3,1,4,2:T(8,128)S(1)} %get-tuple-element.45, f32[128,8,1,1,1,216]{0,5,3,1,4,2:T(8,128)S(1)} %get-tuple-element.44), kind=kOutput, calls=%fused_computation.26 | convolution fusion | flops 9173385216 | bytes 17418240 | tf_op jit(solution)/shard_map/pkbxhs,cqs->pkbcxhq/dot_general | solution.py:141
  269.3 30.0 %subtract_reduce_fusion.3 = (f32[128,8,216]{0,2,1:T(8,128)S(1)}, f32[128,8,216]{0,2,1:T(8,128)S(1)}) fusion(f32[128,8,1,8,2,1,216]{0,6,4,1,3,5,2:T(8,128)S(1)} %convolution_bitcast_fusion.2, f32[128,8,8,216]{0,3,2,1:T(8,128)S(1)} %multiply_reduce_fusion.5, f32[8,216]{1,0:T(8,128)S(1)} %copy-done.44, f32[128,8]{0,1:T(8,128)S(1)} %copy-done.57), kind=kLoop, calls=%fused_computation.65 | loop fusion | flops 20791296 | bytes 23014144 | tf_op jit(solution)/shard_map/reduce_sum | solution.py:145
  312.8 6.1 all-to-all-start.2
  342.0 6.7 multiply_reduce_fusion.1
  348.7 8.1 %multiply_reduce_fusion = f32[8,8,16,8,216]{4,3,2,1,0:T(8,128)} fusion(f32[16,8,216,3]{2,1,3,0:T(8,128)S(1)} %get-tuple-element.64, f32[8,8,3]{2,1,0:T(8,128)S(1)} %copy.450), kind=kLoop, calls=%fused_computation | loop fusion | flops 8847360 | bytes 7410432 | tf_op jit(solution)/shard_map/reduce_sum | solution.py:81
  381.9 11.3 %convolution_bitcast_fusion.3 = f32[128,8,1,8,2,1,216]{0,6,1,3,5,4,2:T(8,128)S(1)} fusion(f32[8,216,216,1,1]{2,1,3,0,4:T(8,128)S(1)} %copy-done.2, f32[128,8,1,1,1,216]{0,5,3,1,4,2:T(8,128)S(1)} %get-tuple-element.43, f32[128,8,1,1,1,216]{0,5,3,1,4,2:T(8,128)S(1)} %get-tuple-element.42), kind=kOutput, calls=%fused_computation.75 | convolution fusion | flops 9173385216 | bytes 17418240 | tf_op jit(solution)/shard_map/pkbxhs,cqs->pkbcxhq/dot_general | solution.py:141
  393.2 30.1 %subtract_reduce_fusion.2 = (f32[128,8,216]{0,2,1:T(8,128)S(1)}, f32[128,8,216]{0,2,1:T(8,128)S(1)}) fusion(f32[128,8,1,8,2,1,216]{0,6,1,3,5,4,2:T(8,128)S(1)} %convolution_bitcast_fusion.3, f32[128,8,8,216]{0,3,2,1:T(8,128)S(1)} %bitcast.546, f32[8,216]{1,0:T(8,128)S(1)} %copy-done.43, f32[128,8]{0,1:T(8,128)S(1)} %copy-done.56), kind=kLoop, calls=%fused_computation.62 | loop fusion | flops 20791296 | bytes 23014144 | tf_op jit(solution)/shard_map/reduce_sum | solution.py:145
  429.2 28.6 %multiply_subtract_fusion.3 = (f32[1,8,128,8,1,1,216]{2,6,1,4,3,5,0:T(8,128)S(1)}, f32[1,8,128,8,1,1,216]{2,6,1,4,3,5,0:T(8,128)S(1)}) fusion(f32[8,128,8,216]{1,3,2,0:T(8,128)} %multiply_reduce_fusion.7, f32[8,128,216]{1,2,0:T(8,128)S(1)} %copy-done.6, f32[8,216]{1,0:T(8,128)S(1)} %copy-done.42, f32[128,8]{0,1:T(8,128)S(1)} %copy-done.55, ...), kind=kLoop, calls=%fused_computation.70 | loop fusion | flops 15925248 | bytes 23014144 | tf_op jit(solution)/shard_map/sub | solution.py:90
  457.9 11.6 %fusion.42 = f32[1,128,8,2,1,216]{1,5,3,2,4,0:T(8,128)S(1)} fusion(f32[8,216,216,1,1]{2,1,0,4,3:T(8,128)S(1)} %copy-done.118, f32[1,8,128,8,1,1,216]{2,6,1,4,3,5,0:T(8,128)S(1)} %get-tuple-element.33, f32[1,8,128,8,1,1,216]{2,6,1,4,3,5,0:T(8,128)S(1)} %get-tuple-element.32), kind=kOutput, calls=%fused_computation.114 | convolution fusion | flops 9176481792 | bytes 17418240 | tf_op jit(solution)/shard_map/pctkxhq,cqs->ptkxhs/dot_general | solution.py:114
  477.9 6.2 mul.4982
  505.3 13.6 %convolution_bitcast_fusion.1 = f32[64,8,2,8,2,1,216]{6,0,4,2,1,3,5:T(8,128)S(1)} fusion(f32[8,216,216,1,1,1]{2,1,5,4,3,0:T(8,128)S(1)} %copy-done, f32[64,8,2,1,1,216]{5,0,3,2,1,4:T(8,128)S(1)} %get-tuple-element.41, f32[64,8,2,1,1,216]{5,0,3,2,1,4:T(8,128)S(1)} %get-tuple-element.40), kind=kOutput, calls=%fused_computation.25 | convolution fusion | flops 9173385216 | bytes 17418240 | tf_op jit(solution)/shard_map/pkbxhs,cqs->pkbcxhq/dot_general | solution.py:141
  518.9 38.7 %subtract_reduce_fusion.1 = (f32[64,2,8,216]{3,0,1,2:T(8,128)}, f32[64,2,8,216]{3,0,1,2:T(8,128)}) fusion(f32[64,8,2,8,2,1,216]{6,0,4,2,1,3,5:T(8,128)S(1)} %convolution_bitcast_fusion.1, f32[64,8,2,8,216]{4,3,2,1,0:T(8,128)S(1)} %bitcast.542, f32[2,8,216]{2,0,1:T(2,128)S(1)} %copy-done.34, f32[64,8]{0,1:T(8,128)S(1)} %copy-done.60), kind=kLoop, calls=%fused_computation.43 | loop fusion | flops 20791296 | bytes 23019008 | tf_op jit(solution)/shard_map/reduce_sum | solution.py:145
  566.6 14.7 %convolution_bitcast_fusion = f32[8,8,16,8,2,1,216]{6,2,4,1,0,3,5:T(8,128)S(1)} fusion(f32[8,216,216,1,1,1]{2,1,5,4,3,0:T(8,128)S(1)} %copy-done.1, f32[8,8,16,1,1,216]{5,2,3,1,0,4:T(8,128)S(1)} %get-tuple-element.37, f32[8,8,16,1,1,216]{5,2,3,1,0,4:T(8,128)S(1)} %get-tuple-element.36), kind=kOutput, calls=%fused_computation.24 | convolution fusion | flops 9173385216 | bytes 17418240 | tf_op jit(solution)/shard_map/pkbxhs,cqs->pkbcxhq/dot_general | solution.py:141
  581.3 37.1 %subtract_reduce_fusion = (f32[8,16,8,216]{3,1,0,2:T(8,128)S(1)}, f32[8,16,8,216]{3,1,0,2:T(8,128)}) fusion(f32[8,8,16,8,2,1,216]{6,2,4,1,0,3,5:T(8,128)S(1)} %convolution_bitcast_fusion, f32[8,8,16,8,216]{4,3,2,1,0:T(8,128)S(1)} %bitcast.544, f32[16,8,216]{2,0,1:T(8,128)S(1)} %copy-done.13, f32[8,8]{1,0:T(8,128)S(1)} %get-tuple-element.136), kind=kLoop, calls=%fused_computation.40 | loop fusion | flops 20791296 | bytes 23113984 | tf_op jit(solution)/shard_map/reduce_sum | solution.py:145
  629.8 6.1 copy.411
  637.8 28.8 %multiply_subtract_fusion.2 = (f32[1,8,128,8,1,1,216]{2,6,1,4,3,5,0:T(8,128)S(1)}, f32[1,8,128,8,1,1,216]{2,6,1,4,3,5,0:T(8,128)S(1)}) fusion(f32[8,128,8,216]{1,3,2,0:T(8,128)} %multiply_reduce_fusion.6, f32[8,128,216]{1,2,0:T(8,128)S(1)} %copy.416, f32[8,216]{1,0:T(8,128)S(1)} %sqrt.134, f32[128,8]{0,1:T(8,128)S(1)} %copy-done.54, f32[8,128,216]{1,2,0:T(8,128)S(1)} %copy.412), kind=kLoop, calls=%fused_computation.68 | loop fusion | flops 15925248 | bytes 23014144 | tf_op jit(solution)/shard_map/sub | solution.py:90
  666.7 11.6 %fusion.41 = f32[1,128,8,2,1,216]{1,5,3,2,4,0:T(8,128)S(1)} fusion(f32[8,216,216,1,1]{2,1,0,4,3:T(8,128)S(1)} %copy-done.119, f32[1,8,128,8,1,1,216]{2,6,1,4,3,5,0:T(8,128)S(1)} %get-tuple-element.31, f32[1,8,128,8,1,1,216]{2,6,1,4,3,5,0:T(8,128)S(1)} %get-tuple-element.30), kind=kOutput, calls=%fused_computation.113 | convolution fusion | flops 9176481792 | bytes 17418240 | tf_op jit(solution)/shard_map/pctkxhq,cqs->ptkxhs/dot_general | solution.py:114
  (533 shorter events, 260.0 us)
Async XLA Ops:
  179.7 41.7 %copy-start.106 = (f32[3]{0:T(128)S(1)}, f32[3]{0:T(128)}, u32[]{:S(2)}) copy-start(f32[3]{0:T(128)} %get-tuple-element.80) | copy-start | bytes 40
  179.7 41.7 %copy-start.107 = (f32[3]{0:T(128)S(1)}, f32[3]{0:T(128)}, u32[]{:S(2)}) copy-start(f32[3]{0:T(128)} %get-tuple-element.82) | copy-start | bytes 40
  185.1 127.7 %all-to-all-start = ((f32[2,512,432]{2,0,1:T(2,128)}), f32[2,512,432]{2,0,1:T(2,128)S(1)}, u32[]{:S(2)}, u32[]{:S(2)}) async-start(f32[2,512,432]{2,0,1:T(2,128)} %reshape.14002), calls=%async_computation | async-start | bytes 4194304 | tf_op jit(solution)/shard_map/all_to_all | solution.py:189
  246.1 58.3 %copy-start.23 = (f32[128,8,3]{0,2,1:T(4,128)}, f32[128,8,3]{0,2,1:T(4,128)S(1)}, u32[]{:S(2)}) copy-start(f32[128,8,3]{0,2,1:T(4,128)S(1)} %copy.413) | copy-start | bytes 36868
  269.1 33.8 %copy-start.86 = (s32[64,8,1,1,1,1]{0,1,5,4,3,2:T(8,128)S(1)}, s32[64,8,1,1,1,1]{0,1,5,4,3,2:T(8,128)}, u32[]{:S(2)}) copy-start(s32[64,8,1,1,1,1]{0,1,5,4,3,2:T(8,128)} %fusion.548) | copy-start | bytes 6148
  269.1 33.8 %copy-start.87 = (s32[64,8,1,1,1,1]{0,1,5,4,3,2:T(8,128)S(1)}, s32[64,8,1,1,1,1]{0,1,5,4,3,2:T(8,128)}, u32[]{:S(2)}) copy-start(s32[64,8,1,1,1,1]{0,1,5,4,3,2:T(8,128)} %fusion.550) | copy-start | bytes 6148
  269.2 33.8 %copy-start.88 = (s32[64,8,1,1,1,1]{0,1,5,4,3,2:T(8,128)S(1)}, s32[64,8,1,1,1,1]{0,1,5,4,3,2:T(8,128)}, u32[]{:S(2)}) copy-start(s32[64,8,1,1,1,1]{0,1,5,4,3,2:T(8,128)} %fusion.552) | copy-start | bytes 6148
  269.2 34.5 %copy-start.95 = (s32[1,1,128,8,1,1]{2,3,5,4,1,0:T(8,128)S(1)}, s32[1,1,128,8,1,1]{2,3,5,4,1,0:T(8,128)}, u32[]{:S(2)}) copy-start(s32[1,1,128,8,1,1]{2,3,5,4,1,0:T(8,128)} %get-tuple-element.106) | copy-start | bytes 12292
  269.2 34.5 %copy-start.96 = (s32[1,1,128,8,1,1]{2,3,5,4,1,0:T(8,128)S(1)}, s32[1,1,128,8,1,1]{2,3,5,4,1,0:T(8,128)}, u32[]{:S(2)}) copy-start(s32[1,1,128,8,1,1]{2,3,5,4,1,0:T(8,128)} %get-tuple-element.107) | copy-start | bytes 12292
  269.2 34.5 %copy-start.97 = (s32[1,1,128,8,1,1]{2,3,5,4,1,0:T(8,128)S(1)}, s32[1,1,128,8,1,1]{2,3,5,4,1,0:T(8,128)}, u32[]{:S(2)}) copy-start(s32[1,1,128,8,1,1]{2,3,5,4,1,0:T(8,128)} %fusion.541) | copy-start | bytes 12292
  269.2 35.2 %copy-start.39 = (f32[216,3]{0,1:T(4,128)S(1)}, f32[216,3]{0,1:T(4,128)}, u32[]{:S(2)}) copy-start(f32[216,3]{0,1:T(4,128)} %get-tuple-element.78) | copy-start | bytes 7780
  269.2 35.2 %copy-start.58 = (f32[216,3]{0,1:T(4,128)S(1)}, f32[216,3]{0,1:T(4,128)}, u32[]{:S(2)}) copy-start(f32[216,3]{0,1:T(4,128)} %get-tuple-element.77) | copy-start | bytes 7780
  269.2 36.8 %copy-start.98 = (s32[1,128,8,1,1]{1,2,4,3,0:T(8,128)S(1)}, s32[1,128,8,1,1]{1,2,4,3,0:T(8,128)}, u32[]{:S(2)}) copy-start(s32[1,128,8,1,1]{1,2,4,3,0:T(8,128)} %get-tuple-element.104) | copy-start | bytes 12292
  269.2 36.8 %copy-start.99 = (s32[1,128,8,1,1]{1,2,4,3,0:T(8,128)S(1)}, s32[1,128,8,1,1]{1,2,4,3,0:T(8,128)}, u32[]{:S(2)}) copy-start(s32[1,128,8,1,1]{1,2,4,3,0:T(8,128)} %get-tuple-element.105) | copy-start | bytes 12292
  269.2 38.3 %copy-start.92 = (s32[1,128,8,1,1]{1,2,4,3,0:T(8,128)S(1)}, s32[1,128,8,1,1]{1,2,4,3,0:T(8,128)}, u32[]{:S(2)}) copy-start(s32[1,128,8,1,1]{1,2,4,3,0:T(8,128)} %get-tuple-element.108) | copy-start | bytes 12292
  269.2 38.3 %copy-start.93 = (s32[1,128,8,1,1]{1,2,4,3,0:T(8,128)S(1)}, s32[1,128,8,1,1]{1,2,4,3,0:T(8,128)}, u32[]{:S(2)}) copy-start(s32[1,128,8,1,1]{1,2,4,3,0:T(8,128)} %get-tuple-element.109) | copy-start | bytes 12292
  269.3 38.3 %copy-start.94 = (s32[1,128,8,1,1]{1,2,4,3,0:T(8,128)S(1)}, s32[1,128,8,1,1]{1,2,4,3,0:T(8,128)}, u32[]{:S(2)}) copy-start(s32[1,128,8,1,1]{1,2,4,3,0:T(8,128)} %fusion.672) | copy-start | bytes 12292
  269.3 39.0 %copy-start.45 = (f32[2,216,3]{1,2,0:T(4,128)S(1)}, f32[2,216,3]{1,2,0:T(4,128)}, u32[]{:S(2)}) copy-start(f32[2,216,3]{1,2,0:T(4,128)} %get-tuple-element.70) | copy-start | bytes 15556
  269.3 40.4 %copy-start.32 = (f32[4]{0:T(128)S(1)}, f32[4]{0:T(128)}, u32[]{:S(2)}) copy-start(f32[4]{0:T(128)} %param.22) | copy-start | bytes 52
  269.3 40.3 %copy-start.61 = (f32[128,8]{0,1:T(8,128)S(1)}, f32[128,8]{0,1:T(8,128)}, u32[]{:S(2)}) copy-start(f32[128,8]{0,1:T(8,128)} %get-tuple-element.127) | copy-start | bytes 12292
  269.3 41.0 %copy-start.62 = (f32[128,8]{0,1:T(8,128)S(1)}, f32[128,8]{0,1:T(8,128)}, u32[]{:S(2)}) copy-start(f32[128,8]{0,1:T(8,128)} %get-tuple-element.129) | copy-start | bytes 12292
  312.8 49.9 %all-to-all-start.2 = ((f32[128,8,432]{0,2,1:T(8,128)}), f32[128,8,432]{0,2,1:T(8,128)}, u32[]{:S(2)}, u32[]{:S(2)}) async-start(f32[128,8,432]{0,2,1:T(8,128)} %bitcast.548), calls=%async_computation.2 | async-start | bytes 3538944 | tf_op jit(solution)/shard_map/all_to_all | solution.py:256
  424.7 59.3 %all-to-all-start.3 = ((f32[128,8,432]{0,2,1:T(8,128)}), f32[128,8,432]{0,2,1:T(8,128)}, u32[]{:S(2)}, u32[]{:S(2)}) async-start(f32[128,8,432]{0,2,1:T(8,128)} %bitcast.113), calls=%async_computation.3 | async-start | bytes 3538944 | tf_op jit(solution)/shard_map/all_to_all | solution.py:209
  484.1 145.7 %all-to-all-start.1 = ((f32[1,1024,432]{2,0,1:T(1,128)}), f32[1,1024,432]{2,0,1:T(1,128)S(1)}, u32[]{:S(2)}, u32[]{:S(2)}) async-start(f32[1,1024,432]{2,0,1:T(1,128)} %mul.4982), calls=%async_computation.1 | async-start | bytes 4194304 | tf_op jit(solution)/shard_map/all_to_all | solution.py:250
  (108 other events, 1551.4 us)
where the time goes:
time: 697 us; the launch traced here: 692 us
  other arithmetic  422 us (61%)
  local copies, waits for them, and re-layouts  131 us (19%)
  matrix products  116 us (17%)
  starting transfers between devices  20 us (3%)
    sub x12, other arithmetic, complex_turn(): real_part * cosine - imag_part * sine_part  159 us
    reduce_sum x4, other arithmetic, adjoint_level(): jnp.sum(back_re, axis=1)  136 us
    dot_general x4, matrix products, forward_level(): jnp.einsum('pctkxhq,cqs->ptkxhs', stacked, interp, precision=lax.Precisio...  65.6 us
    reduce_sum x14, other arithmetic, phase_angle(): along = jnp.sum(centres * points, axis=-1)  56.3 us
    dot_general x4, matrix products, adjoint_level(): jnp.einsum('pkbxhs,cqs->pkbcxhq', stacked, interp, precision=lax.Precisio...  50.9 us
    unnamed x264, local copies, waits for them, and re-layouts  23.4 us
    another operation x42, other arithmetic, box_digits(): return jnp.stack([coord_x, coord_y, coord_z], axis=-1).astype(jnp.float32)  22.7 us
    mul x6, local copies, waits for them, and re-layouts, forward_level(): output = shrink * jnp.stack([result_re, result_im], axis=3)  20.4 us
  transfers between devices with their start and end apart: 4, of which 0 were waited for; matrix products, arithmetic and copies ran while one was open for 52% of the time, Pallas kernels for 0%

commit v1 on v0

v1 whole, which is shorter than its diff:
```python
import math

import jax
import jax.numpy as jnp
import ml_dtypes
import numpy as np
from jax import lax
from jax.experimental import pallas as pl
from jax.experimental.pallas import tpu as pltpu
from jax.sharding import PartitionSpec as P

ORDER = 6
LEVELS = 4
Q = 216
band = 8.0


def cheb_points(n):
    return np.array([(1.0 - math.cos((2 * i + 1) * math.pi / (2 * n))) / 2.0 for i in range(n)])


def child_table(n):
    g = cheb_points(n)
    halves = []
    for bit in range(2):
        m = np.ones((n, n))
        for r in range(n):
            w = (g[r] + bit) / 2.0
            for c in range(n):
                for o in range(n):
                    if o != c:
                        m[r, c] *= (w - g[o]) / (g[c] - g[o])
        halves.append(m)
    return np.stack(
        [np.kron(np.kron(halves[e // 4], halves[e // 2 % 2]), halves[e % 2]) for e in range(8)]
    )


def split_table(table):
    high = table.astype(ml_dtypes.bfloat16)
    low = (table - high.astype(np.float64)).astype(ml_dtypes.bfloat16)
    return jnp.asarray(high), jnp.asarray(low)


def box_coords(index, groups):
    coords = [jnp.zeros_like(index) for _ in range(3)]
    for group in range(groups):
        digit = index // 8 ** (groups - 1 - group) % 8
        bits = (digit // 4, digit // 2 % 2, digit % 2)
        coords = [c * 2 + b for c, b in zip(coords, bits)]
    return [c.astype(jnp.float32) for c in coords]


def point_slopes(src_off, count, groups, medium):
    side = band / float(2**groups)
    g = cheb_points(ORDER).astype(np.float32)
    grid = (np.repeat(g, ORDER * ORDER), np.tile(np.repeat(g, ORDER), ORDER), np.tile(g, ORDER**2))
    corner = box_coords(src_off + jnp.arange(count, dtype=jnp.int32), groups)
    pts = [side * (c[:, None] + o[None, :]) for c, o in zip(corner, grid)]
    radius = jnp.sqrt(pts[0] * pts[0] + pts[1] * pts[1] + pts[2] * pts[2])
    return [p + medium[d + 1] * radius for d, p in enumerate(pts)], medium[0] * radius


def turn_of(u):
    half = jnp.round(2.0 * u)
    y = (2.0 * math.pi) * (u - 0.5 * half)
    sign = 1.0 - 2.0 * (half - 2.0 * jnp.floor(0.5 * half))
    z = y * y
    s = jnp.float32(-1.0 / math.factorial(11))
    for n in (9, 7, 5, 3, 1):
        s = s * z + (1.0 if n % 4 == 1 else -1.0) / math.factorial(n)
    c = jnp.float32(1.0 / math.factorial(12))
    for n in (10, 8, 6, 4, 2, 0):
        c = c * z + (1.0 if n % 4 == 0 else -1.0) / math.factorial(n)
    return sign * c, sign * (s * y)


def pair_phase(src_off, src_count, src_groups, tgt_off, tgt_count, tgt_groups, medium):
    slopes, base = point_slopes(src_off, src_count, src_groups, medium)
    coords = box_coords(tgt_off + jnp.arange(tgt_count, dtype=jnp.int32), tgt_groups)
    u = base[:, None, :]
    for c, a in zip(coords, slopes):
        u = u + ((c + 0.5) / float(2**tgt_groups))[None, :, None] * a[:, None, :]
    return turn_of(u)


def child_phase(src_off, src_count, level, medium):
    slopes, _ = point_slopes(src_off, src_count, LEVELS - level, medium)
    k = np.arange(8)
    u = 0.0
    for bits, a in zip((k // 4, k // 2 % 2, k % 2), slopes):
        step = ((bits - 0.5) / 2.0 ** (level + 2)).astype(np.float32)
        u = u + step[None, :, None] * a[:, None, :]
    return jnp.stack(turn_of(u), axis=1)


def dot3(x, high, low):
    x_high = x.astype(jnp.bfloat16)
    x_low = (x - x_high.astype(jnp.float32)).astype(jnp.bfloat16)
    dot = lambda a, b: jnp.dot(a, b, preferred_element_type=jnp.float32)
    return dot(x_high, high) + dot(x_high, low) + dot(x_low, high)


def forward_kernel(x_ref, w_ref, high_ref, low_ref, o_ref):
    pb, _, _, tb, q = o_ref.shape[0], 2, 8, o_ref.shape[3], o_ref.shape[4]

    def step(e, acc):
        parts = []
        for p in range(pb):
            re, im = x_ref[p, e, 0], x_ref[p, e, 1]
            w_re, w_im = w_ref[p, e, 0], w_ref[p, e, 1]
            res = [re * w_re[k : k + 1] - im * w_im[k : k + 1] for k in range(8)]
            ims = [re * w_im[k : k + 1] + im * w_re[k : k + 1] for k in range(8)]
            parts += res + ims
        return acc + dot3(jnp.concatenate(parts, axis=0), high_ref[e], low_ref[e])

    acc = lax.fori_loop(0, 8, step, jnp.zeros((pb * 16 * tb, q), jnp.float32))
    o_ref[...] = acc.reshape(o_ref.shape)


def adjoint_kernel(y_ref, w_ref, high_ref, low_ref, o_ref):
    sb, tb, q = y_ref.shape[0], y_ref.shape[3], y_ref.shape[4]
    rows = y_ref[...].reshape(sb * 16 * tb, q)

    def step(e, carry):
        z = dot3(rows, high_ref[e], low_ref[e]).reshape(sb, 2, 8, tb, q)
        for s in range(sb):
            w_re, w_im = w_ref[s, e, 0], w_ref[s, e, 1]
            out_re = jnp.zeros((tb, q), jnp.float32)
            out_im = jnp.zeros((tb, q), jnp.float32)
            for k in range(8):
                re, im = z[s, 0, k], z[s, 1, k]
                c, d = w_re[k : k + 1], w_im[k : k + 1]
                out_re += re * c + im * d
                out_im += im * c - re * d
            o_ref[s, e, 0] = out_re
            o_ref[s, e, 1] = out_im
        return carry

    lax.fori_loop(0, 8, step, 0)


def blocks(count, tgt):
    tb = min(tgt, 32)
    return math.gcd(count, max(1, 32 // tb)), tb


def level_call(kernel, operand, phase, tables, out_shape):
    count, tgt, q = operand.shape[0], operand.shape[3], operand.shape[4]
    cb, tb = blocks(count, tgt)
    spec = lambda: pl.BlockSpec((cb, operand.shape[1], operand.shape[2], tb, q), lambda i, j: (i, 0, 0, j, 0))
    return pl.pallas_call(
        kernel,
        grid=(count // cb, tgt // tb),
        in_specs=[
            spec(),
            pl.BlockSpec((cb,) + phase.shape[1:], lambda i, j: (i, 0, 0, 0, 0)),
            pl.BlockSpec(tables[0].shape, lambda i, j: (0, 0, 0)),
            pl.BlockSpec(tables[1].shape, lambda i, j: (0, 0, 0)),
        ],
        out_specs=pl.BlockSpec((cb, out_shape[1], out_shape[2], tb, q), lambda i, j: (i, 0, 0, j, 0)),
        out_shape=jax.ShapeDtypeStruct(out_shape, jnp.float32),
        compiler_params=pltpu.CompilerParams(vmem_limit_bytes=56 * 1024 * 1024),
    )(operand, phase, *tables)


def forward_level(x, src_off, level, medium, tables):
    count, _, tgt, q = x.shape
    phase = child_phase(src_off, count, level, medium).reshape(count // 8, 8, 2, 8, q)
    out = level_call(
        forward_kernel, x.reshape(count // 8, 8, 2, tgt, q), phase, tables, (count // 8, 2, 8, tgt, q)
    )
    return out.swapaxes(2, 3).reshape(count // 8, 2, tgt * 8, q)


def adjoint_level(y, src_off, level, medium, tables):
    count, _, tgt, q = y.shape
    phase = child_phase(src_off * 8, count * 8, level, medium).reshape(count, 8, 2, 8, q)
    operand = y.reshape(count, 2, tgt // 8, 8, q).swapaxes(2, 3)
    out = level_call(adjoint_kernel, operand, phase, tables, (count, 8, 2, tgt // 8, q))
    return out.reshape(count * 8, 2, tgt // 8, q)


def shards(forward_weights, adjoint_weights, medium):
    table = child_table(ORDER) / math.sqrt(8.0)
    forward_tables = split_table(table)
    adjoint_tables = split_table(table.transpose(0, 2, 1))
    sizes = {a: lax.axis_size(a) for a in ("sx", "sy")}
    index = {a: lax.axis_index(a) for a in ("sx", "sy")}
    local_sources = forward_weights.shape[0]
    shots = forward_weights.shape[2] // (2 * Q)
    plan = []
    remaining = ["sx", "sy"]
    width = local_sources
    for _ in range(LEVELS):
        while width < 8:
            axis = remaining.pop(0)
            plan.append(axis)
            width *= sizes[axis]
        plan.append("level")
        width //= 8

    f_in = forward_weights.reshape(local_sources, -1, 2, shots, Q)
    b_in = adjoint_weights.reshape(adjoint_weights.shape[0], 2, shots, Q)
    f_src = (index["sy"] * sizes["sx"] + index["sx"]) * local_sources
    b_tgt = (index["sx"] * sizes["sy"] + index["sy"]) * adjoint_weights.shape[0]
    f_outs, b_outs = [], []
    for shot in range(shots):
        src, tgt, level = f_src, jnp.int32(0), 0
        re, im = f_in[:, :, 0, shot], f_in[:, :, 1, shot]
        c, s = pair_phase(src, re.shape[0], LEVELS, tgt, re.shape[1], 1, medium)
        x = jnp.stack([re * c - im * s, re * s + im * c], axis=1)
        for op in plan:
            if op == "level":
                x = forward_level(x, src, level, medium, forward_tables)
                src, tgt, level = src // 8, tgt * 8, level + 1
            else:
                n = sizes[op]
                count, _, width, _ = x.shape
                x = x.reshape(count, 2, n, width // n, Q).transpose(2, 0, 1, 3, 4)
                x = lax.all_to_all(x, op, split_axis=0, concat_axis=0, tiled=True)
                x = x.reshape(n * count, 2, width // n, Q)
                src = src - index[op] * count
                tgt = tgt + index[op] * (width // n)
        c, s = pair_phase(src, x.shape[0], LEVELS - level, tgt, x.shape[2], level + 1, medium)
        re, im = x[:, 0], x[:, 1]
        f_outs.append((re * c + im * s, im * c - re * s))
        src, tgt, level = jnp.int32(0), b_tgt, LEVELS
        re, im = b_in[None, :, 0, shot], b_in[None, :, 1, shot]
        c, s = pair_phase(src, 1, 0, tgt, re.shape[1], LEVELS + 1, medium)
        y = jnp.stack([re * c - im * s, re * s + im * c], axis=1)
        for op in reversed(plan):
            if op == "level":
                y = adjoint_level(y, src, level - 1, medium, adjoint_tables)
                src, tgt, level = src * 8, tgt // 8, level - 1
            else:
                n = sizes[op]
                count, _, width, _ = y.shape
                y = y.reshape(n, count // n, 2, width, Q)
                y = lax.all_to_all(y, op, split_axis=0, concat_axis=0, tiled=True)
                y = y.transpose(1, 2, 0, 3, 4).reshape(count // n, 2, n * width, Q)
                src = src + index[op] * (count // n)
                tgt = tgt - index[op] * width
        c, s = pair_phase(src, y.shape[0], LEVELS, tgt, y.shape[2], 1, medium)
        re, im = y[:, 0], y[:, 1]
        b_outs.append((re * c + im * s, im * c - re * s))
    f = jnp.stack([jnp.stack([o[i][0] for o in f_outs], axis=1) for i in range(2)], axis=1)
    b = jnp.stack([jnp.stack([o[i].swapaxes(0, 1) for o in b_outs], axis=2) for i in range(2)], axis=2)
    return f.reshape(f.shape[0], -1), b.reshape(b.shape[0], b.shape[1], -1)


def solution(mesh):
    in_specs = (P(("sy", "sx"), None, None), P(("sx", "sy"), None), P())
    out_specs = (P(("sx", "sy"), None), P(None, ("sy", "sx"), None))
    return jax.shard_map(shards, mesh=mesh, in_specs=in_specs, out_specs=out_specs, check_vma=False)
```

time: 697 us -> 276 us (0.40)
  other arithmetic: 422 us -> 41.6 us
  Pallas kernels: 0 us -> 123 us
  matrix products: 116 us -> 0 us
  local copies, waits for them, and re-layouts: 131 us -> 50.7 us
  waiting for transfers between devices: 0.01 us -> 36.6 us
    reduce_sum x44 -> x0, other arithmetic: 209 us -> none  [the longest x4 136 us: adjoint_level(): jnp.sum(back_re, axis=1)]
    sub x12 -> x1, other arithmetic: 159 us -> 3.09 us  [shards(): y = jnp.stack([re * c - im * s, re * s + im * c], axis=1)]
    pallas_call x0 -> x8, Pallas kernels: none -> 123 us  [level_call(): pl.pallas_call(kernel, grid=(count // cb, tgt // tb), in_specs=[spec(), p...]
    dot_general x8 -> x0, matrix products: 116 us -> none  [the longest x4 65.6 us: forward_level(): jnp.einsum('pctkxhq,cqs->ptkxhs', stacked, interp, precision=lax.Precisio...]
    all_to_all x4, waiting for transfers between devices: 0.01 us -> 36.6 us  [the longest x2 18.8 us: shards(): x = lax.all_to_all(x, op, split_axis=0, concat_axis=0, tiled=True)]
    mul x17 -> x0, local copies, waits for them, and re-layouts: 35.2 us -> none  [the longest x6 20.4 us: forward_level(): output = shrink * jnp.stack([result_re, result_im], axis=3)]
    unnamed x264 -> x74, local copies, waits for them, and re-layouts: 23.4 us -> 5.12 us
    transpose x0 -> x7, local copies, waits for them, and re-layouts: none -> 17.6 us  [the longest x4 12.3 us: forward_level(): return out.swapaxes(2, 3).reshape(count // 8, 2, tgt * 8, q)]
  transfers between devices with their start and end apart: 4 -> 4, of which waited for: 0 -> 2; matrix products, arithmetic and copies ran while one was open for 52% -> 19% of each run, Pallas kernels for 0% -> 23%
where the time goes in v1:
time: 276 us; the launch traced here: 273 us
  Pallas kernels  123 us (45%)
  local copies, waits for them, and re-layouts  50.7 us (18%)
  other arithmetic  41.6 us (15%)
  waiting for transfers between devices  36.6 us (13%)
  starting transfers between devices  19.9 us (7%)
    pallas_call x8, Pallas kernels, level_call(): pl.pallas_call(kernel, grid=(count // cb, tgt // tb), in_specs=[spec(), p...  123 us
    all_to_all x2, waiting for transfers between devices, shards(): x = lax.all_to_all(x, op, split_axis=0, concat_axis=0, tiled=True)  18.8 us
    all_to_all x2, waiting for transfers between devices, shards(): y = lax.all_to_all(y, op, split_axis=0, concat_axis=0, tiled=True)  17.8 us
    transpose x4, local copies, waits for them, and re-layouts, forward_level(): return out.swapaxes(2, 3).reshape(count // 8, 2, tgt * 8, q)  12.3 us
    all_to_all x2, starting transfers between devices, shards(): y = lax.all_to_all(y, op, split_axis=0, concat_axis=0, tiled=True)  10.3 us
    all_to_all x2, starting transfers between devices, shards(): x = lax.all_to_all(x, op, split_axis=0, concat_axis=0, tiled=True)  9.58 us
    another operation x3, local copies, waits for them, and re-layouts, adjoint_level(): operand = y.reshape(count, 2, tgt // 8, 8, q).swapaxes(2, 3)  7.79 us
    mul x4, other arithmetic, turn_of(): return (sign * c, sign * (s * y))  7.19 us
  transfers between devices with their start and end apart: 4, of which 2 were waited for; matrix products, arithmetic and copies ran while one was open for 19% of the time, Pallas kernels for 23%

profile of v1, /device:TPU:1, one launch (start us, length us, event | category | flops | bytes accessed | tf_op | source)
XLA Modules:
  0.0 273.4 jit_solution(4529691224481224079)
XLA Ops:
  8.0 5.5 %fusion.16 = (f32[16,8,1,8,216]{4,3,2,1,0:T(8,128)}, f32[16,8,1,8,216]{4,3,2,1,0:T(8,128)}, f32[16,8,1,8,216]{4,3,2,1,0:T(8,128)S(1)}, f32[16,8,1,8,216]{4,3,2,1...) fusion(f32[16,8,216]{2,1,0:T(8,128)S(1)} %get-tuple-element.25, ...), kind=kLoop, calls=%fused_computation.54 | loop fusion | flops 28753920 | bytes 7852224 | tf_op jit(solution)/shard_map/mul | solution.py:75
  16.6 16.0 %shard_map.626 = f32[16,2,8,8,216]{4,3,2,1,0:T(8,128)} custom-call(f32[16,8,2,8,216]{4,3,2,1,0:T(8,128)} %pad_maximum_fusion.x_ref, f32[16,8,2,8,216]{4,3,2,1,0:T(8,128)} %pad_maximum_fusion.1.w_ref, bf16[8,216,216]{2,1,0:T(8,128)(2,1)} %constant.1564.clone.high_ref, bf16[8,216,216]{2,1,0:T(8,128)(2,1)} %constant.1565.clone.low_ref), custom_call_target="tpu_custom_call" | custom-call | tf_op jit(solution)/shard_map/pallas_call | solution.py:152
  32.6 3.9 %copy.147 = f32[16,2,8,8,216]{4,3,2,1,0:T(8,128)} copy(f32[16,2,8,8,216]{4,2,3,1,0:T(8,128)} %bitcast.112) | data formatting | bytes 3538944 | tf_op jit(solution)/shard_map/transpose | solution.py:173
  40.2 16.0 %shard_map.627 = f32[2,2,8,64,216]{4,3,2,1,0:T(8,128)} custom-call(f32[2,8,2,64,216]{4,3,2,1,0:T(8,128)} %bitcast.94, f32[2,8,2,8,216]{4,3,2,1,0:T(8,128)} %pad_maximum_fusion.5.w_ref, bf16[8,216,216]{2,1,0:T(8,128)(2,1)} %constant.1564.clone.high_ref, bf16[8,216,216]{2,1,0:T(8,128)(2,1)} %constant.1565.clone.low_ref), custom_call_target="tpu_custom_call" | custom-call | tf_op jit(solution)/shard_map/pallas_call | solution.py:152
  60.8 4.4 %all-to-all-start = ((f32[4,2,2,128,216]{3,4,2,1,0:T(8,128)}), f32[4,2,2,128,216]{3,4,2,1,0:T(8,128)S(1)}, u32[]{:S(2)}, u32[]{:S(2)}) async-start(f32[4,2,2,128,216]{3,4,2,1,0:T(8,128)} %copy.149), calls=%async_computation | async-start | bytes 3538944 | tf_op jit(solution)/shard_map/all_to_all | solution.py:221
  79.8 3.1 %multiply_subtract_fusion.2 = (f32[1,1,128,8,216]{4,2,3,1,0:T(8,128)S(1)}, f32[1,1,128,8,216]{4,2,3,1,0:T(8,128)S(1)}) fusion(f32[1,1,128,8,216]{4,3,2,1,0:T(8,128)S(1)} %bitcast.113, f32[1,1,128,8,216]{4,3,2,1,0:T(8,128)} %bitcast.114, f32[216]{0:T(256)S(1)} %bitcast.123, f32[128,8]{0,1:T(8,128)S(1)} %fusion.321, f32[216]{0:T(256)S(1)} %bitcast.125, ...), kind=kLoop, calls=%fused_computation.63 | loop fusion | flops 10616832 | bytes 3554688 | tf_op jit(solution)/shard_map/sub | solution.py:231
  84.4 14.8 %shard_map.630 = f32[1,8,2,128,216]{4,3,2,1,0:T(8,128)} custom-call(f32[1,2,8,128,216]{4,3,2,1,0:T(8,128)} %maximum_bitcast_fusion.y_ref, f32[1,8,2,8,216]{4,3,2,1,0:T(8,128)} %maximum_bitcast_fusion.3.w_ref, bf16[8,216,216]{2,1,0:T(8,128)(2,1)} %constant.1566.clone.high_ref, bf16[8,216,216]{2,1,0:T(8,128)(2,1)} %constant.1567.clone.low_ref), custom_call_target="tpu_custom_call" | custom-call | tf_op jit(solution)/shard_map/pallas_call | solution.py:152
  99.2 2.8 %copy.165 = f32[8,1,2,128,216]{3,4,2,1,0:T(8,128)} copy(f32[8,1,2,128,216]{4,3,2,0,1:T(8,128)} %bitcast.102) | data formatting | bytes 3538944 | tf_op jit(solution)/shard_map/reshape;reshape | solution.py:239
  102.1 5.9 %all-to-all-start.2 = ((f32[8,1,2,128,216]{3,4,2,1,0:T(8,128)}), f32[8,1,2,128,216]{3,4,2,1,0:T(8,128)}, u32[]{:S(2)}, u32[]{:S(2)}) async-start(f32[8,1,2,128,216]{3,4,2,1,0:T(8,128)} %copy.165), calls=%async_computation.2 | async-start | bytes 3538944 | tf_op jit(solution)/shard_map/all_to_all | solution.py:240
  110.8 16.0 %shard_map.628 = f32[1,2,8,128,216]{4,3,2,1,0:T(8,128)} custom-call(f32[1,8,2,128,216]{4,3,2,1,0:T(8,128)} %bitcast.103, f32[1,8,2,8,216]{4,3,2,1,0:T(8,128)} %maximum_bitcast_fusion.1.w_ref, bf16[8,216,216]{2,1,0:T(8,128)(2,1)} %constant.1564.clone.high_ref, bf16[8,216,216]{2,1,0:T(8,128)(2,1)} %constant.1565.clone.low_ref), custom_call_target="tpu_custom_call" | custom-call | tf_op jit(solution)/shard_map/pallas_call | solution.py:152
  126.8 2.8 %copy.151 = f32[1,2,128,8,216]{4,3,2,1,0:T(8,128)S(1)} copy(f32[1,2,128,8,216]{4,2,3,1,0:T(8,128)} %bitcast.97) | data formatting | bytes 3538944 | tf_op jit(solution)/shard_map/transpose | solution.py:173
  131.4 17.8 %all-to-all-done.2 = f32[8,1,2,128,216]{3,4,2,1,0:T(8,128)} async-done(((f32[8,1,2,128,216]{3,4,2,1,0:T(8,128)}), f32[8,1,2,128,216]{3,4,2,1,0:T(8,128)}, u32[]{:S(2)}, u32[]{:S(2)}) %all-to-all-start.2) | async-done | bytes 1769504 | tf_op jit(solution)/shard_map/all_to_all | solution.py:240
  149.2 5.2 %all-to-all-start.1 = ((f32[8,1,2,128,216]{3,4,2,1,0:T(8,128)}), f32[8,1,2,128,216]{3,4,2,1,0:T(8,128)}, u32[]{:S(2)}, u32[]{:S(2)}) async-start(f32[8,1,2,128,216]{3,4,2,1,0:T(8,128)} %copy.152), calls=%async_computation.1 | async-start | bytes 3538944 | tf_op jit(solution)/shard_map/all_to_all | solution.py:221
  159.1 14.8 %shard_map.631 = f32[1,8,2,128,216]{4,3,2,1,0:T(8,128)} custom-call(f32[1,2,8,128,216]{4,3,2,1,0:T(8,128)} %bitcast.98, f32[1,8,2,8,216]{4,3,2,1,0:T(8,128)} %maximum_bitcast_fusion.4.w_ref, bf16[8,216,216]{2,1,0:T(8,128)(2,1)} %constant.1566.clone.high_ref, bf16[8,216,216]{2,1,0:T(8,128)(2,1)} %constant.1567.clone.low_ref), custom_call_target="tpu_custom_call" | custom-call | tf_op jit(solution)/shard_map/pallas_call | solution.py:152
  173.9 2.8 %copy.168 = f32[4,2,2,128,216]{3,4,2,1,0:T(8,128)} copy(f32[4,2,2,128,216]{4,3,2,1,0:T(8,128)} %bitcast.104) | data formatting | bytes 3538944 | tf_op jit(solution)/shard_map/reshape;reshape | solution.py:239
  176.7 18.8 %all-to-all-done.1 = f32[8,1,2,128,216]{3,4,2,1,0:T(8,128)} async-done(((f32[8,1,2,128,216]{3,4,2,1,0:T(8,128)}), f32[8,1,2,128,216]{3,4,2,1,0:T(8,128)}, u32[]{:S(2)}, u32[]{:S(2)}) %all-to-all-start.1) | async-done | bytes 1769504 | tf_op jit(solution)/shard_map/all_to_all | solution.py:221
  195.5 4.4 %all-to-all-start.3 = ((f32[4,2,2,128,216]{3,4,2,1,0:T(8,128)}), f32[4,2,2,128,216]{3,4,2,1,0:T(8,128)}, u32[]{:S(2)}, u32[]{:S(2)}) async-start(f32[4,2,2,128,216]{3,4,2,1,0:T(8,128)} %copy.168), calls=%async_computation.3 | async-start | bytes 3538944 | tf_op jit(solution)/shard_map/all_to_all | solution.py:240
  205.5 2.9 %copy.153 = f32[8,1,2,128,216]{4,3,2,0,1:T(8,128)} copy(f32[8,1,2,128,216]{3,4,2,1,0:T(8,128)} %all-to-all-done.1) | data formatting | bytes 3538944 | tf_op jit(solution)/shard_map/all_to_all | solution.py:221
  208.4 16.0 %shard_map.629 = f32[1,2,8,128,216]{4,3,2,1,0:T(8,128)} custom-call(f32[1,8,2,128,216]{4,3,2,1,0:T(8,128)} %bitcast.101, f32[1,8,2,8,216]{4,3,2,1,0:T(8,128)} %maximum_bitcast_fusion.2.w_ref, bf16[8,216,216]{2,1,0:T(8,128)(2,1)} %constant.1564.clone.high_ref, bf16[8,216,216]{2,1,0:T(8,128)(2,1)} %constant.1565.clone.low_ref), custom_call_target="tpu_custom_call" | custom-call | tf_op jit(solution)/shard_map/pallas_call | solution.py:152
  224.4 2.8 %copy.190 = f32[1,2,128,8,216]{4,3,2,1,0:T(8,128)S(1)} copy(f32[1,2,128,8,216]{4,2,3,1,0:T(8,128)} %bitcast.95) | data formatting | bytes 3538944 | tf_op jit(solution)/shard_map/transpose | solution.py:173
  234.8 14.9 %shard_map.632 = f32[2,8,2,64,216]{4,3,2,1,0:T(8,128)} custom-call(f32[2,2,8,64,216]{4,3,2,1,0:T(8,128)} %bitcast.99, f32[2,8,2,8,216]{4,3,2,1,0:T(8,128)} %pad_maximum_fusion.6.w_ref, bf16[8,216,216]{2,1,0:T(8,128)(2,1)} %constant.1566.clone.high_ref, bf16[8,216,216]{2,1,0:T(8,128)(2,1)} %constant.1567.clone.low_ref), custom_call_target="tpu_custom_call" | custom-call | tf_op jit(solution)/shard_map/pallas_call | solution.py:152
  249.7 3.8 %copy.187 = f32[16,2,8,8,216]{4,2,3,1,0:T(8,128)} copy(f32[16,2,8,8,216]{4,3,2,1,0:T(8,128)} %bitcast.100) | data formatting | bytes 3538944 | tf_op jit(solution)/shard_map/reshape;reshape | solution.py:179
  253.6 14.9 %shard_map.633 = f32[16,8,2,8,216]{4,3,2,1,0:T(8,128)} custom-call(f32[16,2,8,8,216]{4,3,2,1,0:T(8,128)} %bitcast.111, f32[16,8,2,8,216]{4,3,2,1,0:T(8,128)} %pad_maximum_fusion.3.w_ref, bf16[8,216,216]{2,1,0:T(8,128)(2,1)} %constant.1566.clone.high_ref, bf16[8,216,216]{2,1,0:T(8,128)(2,1)} %constant.1567.clone.low_ref), custom_call_target="tpu_custom_call" | custom-call | tf_op jit(solution)/shard_map/pallas_call | solution.py:152
  268.4 3.0 %add_bitcast_fusion = (f32[8,128,1,1,216]{4,0,1,3,2:T(8,128)S(1)}, f32[8,128,1,1,216]{4,0,1,3,2:T(8,128)S(1)}) fusion(f32[128,2,8,216]{3,2,1,0:T(8,128)} %bitcast.110, f32[128,216]{1,0:T(8,128)S(1)} %get-tuple-element.48, f32[8]{0:T(128)S(1)} %get-tuple-element.128, f32[128,216]{1,0:T(8,128)S(1)} %get-tuple-element.47, f32[8]{0:T(128)S(1)} %get-tuple-element.127, ...), kind=kLoop, calls=%fused_computation.15 | loop fusion | flops 10616832 | bytes 3981408 | tf_op jit(solution)/shard_map/stack;stack | solution.py:248
  (132 shorter events, 58.8 us)
Async XLA Ops:
  32.6 5.8 %copy-start.32 = (f32[8]{0:T(128)S(1)}, f32[8]{0:T(128)}, u32[]{:S(2)}) copy-start(f32[8]{0:T(128)} %constant.1591) | copy-start | bytes 100
  32.6 5.8 %copy-start.33 = (f32[8]{0:T(128)S(1)}, f32[8]{0:T(128)}, u32[]{:S(2)}) copy-start(f32[8]{0:T(128)} %constant.1590) | copy-start | bytes 100
  32.6 5.8 %copy-start.34 = (f32[8]{0:T(128)S(1)}, f32[8]{0:T(128)}, u32[]{:S(2)}) copy-start(f32[8]{0:T(128)} %constant.1589) | copy-start | bytes 100
  60.8 8.0 %copy-start.2 = (f32[1024,432]{0,1:T(8,128)S(1)}, f32[1024,432]{0,1:T(8,128)}, u32[]{:S(2)}) copy-start(f32[1024,432]{0,1:T(8,128)} %param.68) | copy-start | bytes 5308420
  60.8 41.3 %all-to-all-start = ((f32[4,2,2,128,216]{3,4,2,1,0:T(8,128)}), f32[4,2,2,128,216]{3,4,2,1,0:T(8,128)S(1)}, u32[]{:S(2)}, u32[]{:S(2)}) async-start(f32[4,2,2,128,216]{3,4,2,1,0:T(8,128)} %copy.149), calls=%async_computation | async-start | bytes 3538944 | tf_op jit(solution)/shard_map/all_to_all | solution.py:221
  70.1 4.3 %copy-start.25 = (f32[8]{0:T(128)S(1)}, f32[8]{0:T(128)}, u32[]{:S(2)}) copy-start(f32[8]{0:T(128)} %get-tuple-element.116) | copy-start | bytes 100
  70.1 4.3 %copy-start.26 = (f32[8]{0:T(128)S(1)}, f32[8]{0:T(128)}, u32[]{:S(2)}) copy-start(f32[8]{0:T(128)} %get-tuple-element.121) | copy-start | bytes 100
  70.2 6.2 %copy-start.16 = (f32[8]{0:T(128)S(1)}, f32[8]{0:T(128)}, u32[]{:S(2)}) copy-start(f32[8]{0:T(128)} %constant.1597) | copy-start | bytes 100
  70.2 6.2 %copy-start.17 = (f32[8]{0:T(128)S(1)}, f32[8]{0:T(128)}, u32[]{:S(2)}) copy-start(f32[8]{0:T(128)} %constant.1596) | copy-start | bytes 100
  70.2 6.2 %copy-start.18 = (f32[8]{0:T(128)S(1)}, f32[8]{0:T(128)}, u32[]{:S(2)}) copy-start(f32[8]{0:T(128)} %constant.1595) | copy-start | bytes 100
  70.2 7.1 %copy-start.9 = (f32[1,216]{1,0:T(1,128)S(1)}, f32[1,216]{1,0:T(1,128)}, u32[]{:S(2)}) copy-start(f32[1,216]{1,0:T(1,128)} %constant.1607) | copy-start | bytes 2596
  70.2 7.1 %copy-start.10 = (f32[1,216]{1,0:T(1,128)S(1)}, f32[1,216]{1,0:T(1,128)}, u32[]{:S(2)}) copy-start(f32[1,216]{1,0:T(1,128)} %constant.1610) | copy-start | bytes 2596
  70.3 7.1 %copy-start.11 = (f32[1,216]{1,0:T(1,128)S(1)}, f32[1,216]{1,0:T(1,128)}, u32[]{:S(2)}) copy-start(f32[1,216]{1,0:T(1,128)} %constant.1609) | copy-start | bytes 2596
  70.3 7.1 %copy-start.12 = (f32[1,216]{1,0:T(1,128)S(1)}, f32[1,216]{1,0:T(1,128)}, u32[]{:S(2)}) copy-start(f32[1,216]{1,0:T(1,128)} %constant.1608) | copy-start | bytes 2596
  102.1 6.0 %copy-start.13 = (f32[8]{0:T(128)S(1)}, f32[8]{0:T(128)}, u32[]{:S(2)}) copy-start(f32[8]{0:T(128)} %constant.1594) | copy-start | bytes 100
  102.1 6.0 %copy-start.14 = (f32[8]{0:T(128)S(1)}, f32[8]{0:T(128)}, u32[]{:S(2)}) copy-start(f32[8]{0:T(128)} %constant.1593) | copy-start | bytes 100
  102.1 6.0 %copy-start.15 = (f32[8]{0:T(128)S(1)}, f32[8]{0:T(128)}, u32[]{:S(2)}) copy-start(f32[8]{0:T(128)} %constant.1592) | copy-start | bytes 100
  102.1 47.1 %all-to-all-start.2 = ((f32[8,1,2,128,216]{3,4,2,1,0:T(8,128)}), f32[8,1,2,128,216]{3,4,2,1,0:T(8,128)}, u32[]{:S(2)}, u32[]{:S(2)}) async-start(f32[8,1,2,128,216]{3,4,2,1,0:T(8,128)} %copy.165), calls=%async_computation.2 | async-start | bytes 3538944 | tf_op jit(solution)/shard_map/all_to_all | solution.py:240
  149.2 46.4 %all-to-all-start.1 = ((f32[8,1,2,128,216]{3,4,2,1,0:T(8,128)}), f32[8,1,2,128,216]{3,4,2,1,0:T(8,128)}, u32[]{:S(2)}, u32[]{:S(2)}) async-start(f32[8,1,2,128,216]{3,4,2,1,0:T(8,128)} %copy.152), calls=%async_computation.1 | async-start | bytes 3538944 | tf_op jit(solution)/shard_map/all_to_all | solution.py:221
  176.7 23.9 %copy-start.3 = (f32[2,8,1,8,216]{4,3,2,1,0:T(8,128)S(1)}, f32[2,8,1,8,216]{4,3,2,1,0:T(8,128)}, u32[]{:S(2)}) copy-start(f32[2,8,1,8,216]{4,3,2,1,0:T(8,128)} %get-tuple-element.20) | copy-start | bytes 331780
  176.7 23.9 %copy-start.4 = (f32[2,8,1,8,216]{4,3,2,1,0:T(8,128)S(1)}, f32[2,8,1,8,216]{4,3,2,1,0:T(8,128)}, u32[]{:S(2)}) copy-start(f32[2,8,1,8,216]{4,3,2,1,0:T(8,128)} %get-tuple-element.21) | copy-start | bytes 331780
  176.7 24.6 %copy-start = (f32[16,8,1,8,216]{4,3,2,1,0:T(8,128)S(1)}, f32[16,8,1,8,216]{4,3,2,1,0:T(8,128)}, u32[]{:S(2)}) copy-start(f32[16,8,1,8,216]{4,3,2,1,0:T(8,128)} %get-tuple-element.14) | copy-start | bytes 2654212
  176.7 24.6 %copy-start.1 = (f32[16,8,1,8,216]{4,3,2,1,0:T(8,128)S(1)}, f32[16,8,1,8,216]{4,3,2,1,0:T(8,128)}, u32[]{:S(2)}) copy-start(f32[16,8,1,8,216]{4,3,2,1,0:T(8,128)} %get-tuple-element.15) | copy-start | bytes 2654212
  195.5 35.4 %all-to-all-start.3 = ((f32[4,2,2,128,216]{3,4,2,1,0:T(8,128)}), f32[4,2,2,128,216]{3,4,2,1,0:T(8,128)}, u32[]{:S(2)}, u32[]{:S(2)}) async-start(f32[4,2,2,128,216]{3,4,2,1,0:T(8,128)} %copy.168), calls=%async_computation.3 | async-start | bytes 3538944 | tf_op jit(solution)/shard_map/all_to_all | solution.py:240
  (15 other events, 52.8 us)
